TPU v7x, 256 devices: a whole 4x4x8 slice. The times are simulated.
256 devices in a mesh: replica: 8 (over z_lo, x), fsdp: 32 (over z_hi, y, core).
Axes of the slice: x: 4, y: 4, z: 8 (z_hi: 4, z_lo: 2; z = z_hi * 2 + z_lo), core: 2. Of those that a mesh axis runs over, the one named last changes fastest.
Arguments:
- counts: int32 [8], P('replica'), may hold values from 100 to 1000
- inner: bfloat16 [8, 3, 2, 8192, 1024], P('replica', None, None, 'fsdp'), may hold values from -6 to 6
- anchor: bfloat16 [3, 2, 8192, 1024], P(None, None, 'fsdp'), may hold values from -6 to 6
- momentum: float32 [3, 2, 8192, 1024], P(None, None, ('fsdp', 'replica')), may hold values from -6 to 6
Outputs:
- new_weights: bfloat16 [3, 2, 8192, 1024], P(None, None, 'fsdp')
- new_momentum: float32 [3, 2, 8192, 1024], P(None, None, ('fsdp', 'replica'))
Inputs may be any that keep to these rules, and one draw needn't show every extreme that they name: `counts`: inner steps of a group.
All inputs are finite; a program needn't handle non-finite values.
Results may differ from a plain program's by a relative error of at most 0.001.
Values may be sent and summed in bfloat16 or wider, within the bound.
A program may use at most 128 MiB of HBM per device.

v0:
```python
import jax
import jax.numpy as jnp
from jax import lax
from jax.sharding import PartitionSpec as P

LAYERS = 3


outer_rate = 0.7
momentum_rate = 0.9


def on_device(counts, inner, anchor, momentum):
    total = lax.psum(counts[0], "replica").astype(jnp.float32)
    share = counts[0].astype(jnp.float32) / total
    owned_rows = momentum.shape[2]
    start = lax.axis_index("replica") * owned_rows
    weight_list = []
    moment_list = []
    for layer in range(LAYERS):
        base = anchor[layer].astype(jnp.float32)
        term = share * (base - inner[0, layer].astype(jnp.float32))
        pseudo = lax.psum(term, "replica")
        moment_full = lax.all_gather(momentum[layer], "replica", axis=1, tiled=True)
        moment_next = momentum_rate * moment_full + pseudo
        weights_next = (base - outer_rate * (pseudo + momentum_rate * moment_next)).astype(
            jnp.bfloat16
        )
        moment_list.append(lax.dynamic_slice_in_dim(moment_next, start, owned_rows, 1))
        weight_list.append(weights_next)
    return (jnp.stack(weight_list), jnp.stack(moment_list))


def solution(mesh):
    placed = (
        P("replica"),
        P("replica", None, None, "fsdp", None),
        P(None, None, "fsdp", None),
        P(None, None, ("fsdp", "replica"), None),
    )
    return jax.shard_map(
        on_device,
        mesh=mesh,
        in_specs=placed,
        out_specs=(P(None, None, "fsdp", None), P(None, None, ("fsdp", "replica"), None)),
        check_vma=False,
    )
```

profile of v0, /device:TPU:8, one launch (start us, length us, event | category | flops | bytes accessed | tf_op | source)
XLA Modules:
  0.0 314.4 jit_solution(1849387459540233903)
XLA Ops:
  7.2 0.0 all-gather.11.cloned.1.call-start
  7.2 2.0 fusion.9
  9.2 0.0 all-gather.11.cloned.1.call-update
  9.2 0.0 all-reduce.3.cloned.1.call-start
  9.3 13.1 %psum.28 = s32[]{:T(128)} all-reduce(s32[]{:T(128)} %bitcast.1), channel_id=1, replica_groups=mesh['replica'=8,'fsdp'=32] {'replica'}, use_global_device_ids=true, to_apply=%region_0.0 | all-reduce | flops 1 | bytes 8 | tf_op jit(solution)/shard_map/psum | solution.py:14
  23.8 6.1 %fusion = (f32[2,256,1024]{2,1,0:T(8,128)}, f32[2,256,1024]{2,1,0:T(8,128)}, f32[2,256,1024]{2,1,0:T(8,128)}) fusion(bf16[1,3,2,256,1024]{4,3,2,1,0:T(8,128)(2,1)} %param.5, f32[]{:T(128)S(6)} %div.3, bf16[3,2,256,1024]{3,2,1,0:T(8,128)(2,1)} %param.6), kind=kLoop, calls=%fused_computation.7 | loop fusion | flops 6291456 | bytes 12582916 | tf_op jit(solution)/shard_map/mul | solution.py:22
  29.9 0.0 copy-start
  29.9 0.0 all-reduce.3.cloned.1.call-update
  29.9 0.0 all-gather.9.cloned.1.call-start
  30.0 0.7 all-gather.9.cloned.1.call-update
  30.7 0.0 all-gather.7.cloned.1.call-start
  30.7 0.5 all-gather.7.cloned.1.call-update
  31.3 25.7 %all-gather.11.cloned.1.call-done = f32[1,2,256,1024]{3,2,1,0:T(8,128)} async-done(((f32[1,2,32,1024]{3,2,1,0:T(8,128)}), f32[1,2,256,1024]{3,2,1,0:T(8,128)}) %all-gather.11.cloned.1.call-update) | async-done | bytes 2097168 | tf_op jit(solution)/shard_map/all_gather | solution.py:24
  57.0 153.2 %all-reduce.3.cloned.1.call-done = (f32[2,256,1024]{2,1,0:T(8,128)}, f32[2,256,1024]{2,1,0:T(8,128)}, f32[2,256,1024]{2,1,0:T(8,128)}) async-done(((f32[2,256,1024]{2,1,0:T(8,128)}, f32[2,256,1024]{2,1,0:T(8,128)}, f32[2,256,1024]{2,1,0:T(8,128)}), (f32[2,256,1024]{2,1,0:T(8,128)}, f32[2,256,1024]{2,1,0:T(8,128)}, f32[2,256,1024]{2,1,0:T(8,128)})) %all-reduce.3.cloned.1.call-update) | async-done | bytes 6291472 | tf_op jit(solution)/shard_map/psum | solution.py:23
  210.2 0.0 copy-done
  210.2 3.8 %bitcast_add_fusion = (f32[2,256,1024]{2,1,0:T(8,128)S(1)}, bf16[1,2,256,1024]{3,2,1,0:T(8,128)(2,1)}) fusion(f32[2,256,1024]{2,1,0:T(8,128)} %get-tuple-element.2, f32[1,2,256,1024]{3,2,1,0:T(8,128)} %all-gather.11.cloned.1.call-done, bf16[3,2,256,1024]{3,2,1,0:T(8,128)(2,1)S(1)} %copy-done), kind=kLoop, calls=%fused_computation.13 | loop fusion | flops 4194304 | bytes 8388608 | tf_op jit(solution)/shard_map/add | solution.py:25
  214.1 41.2 %all-gather.9.cloned.1.call-done = f32[1,2,256,1024]{3,2,1,0:T(8,128)} async-done(((f32[1,2,32,1024]{3,2,1,0:T(8,128)}), f32[1,2,256,1024]{3,2,1,0:T(8,128)}) %all-gather.9.cloned.1.call-update) | async-done | bytes 2097168 | tf_op jit(solution)/shard_map/all_gather | solution.py:24
  255.3 3.9 %bitcast_add_fusion.1 = (f32[2,256,1024]{2,1,0:T(8,128)S(1)}, bf16[1,2,256,1024]{3,2,1,0:T(8,128)(2,1)}) fusion(f32[2,256,1024]{2,1,0:T(8,128)} %get-tuple-element.3, f32[1,2,256,1024]{3,2,1,0:T(8,128)} %all-gather.9.cloned.1.call-done, bf16[3,2,256,1024]{3,2,1,0:T(8,128)(2,1)S(1)} %copy-done), kind=kLoop, calls=%fused_computation.14 | loop fusion | flops 4194304 | bytes 8388608 | tf_op jit(solution)/shard_map/add | solution.py:25
  259.1 0.7 dynamic-slice_bitcast_fusion.1
  259.9 41.0 %all-gather.7.cloned.1.call-done = f32[1,2,256,1024]{3,2,1,0:T(8,128)} async-done(((f32[1,2,32,1024]{3,2,1,0:T(8,128)}), f32[1,2,256,1024]{3,2,1,0:T(8,128)}) %all-gather.7.cloned.1.call-update) | async-done | bytes 2097168 | tf_op jit(solution)/shard_map/all_gather | solution.py:24
  300.9 0.0 copy-start.3
  300.9 3.1 bitcast_add_fusion.2
  304.0 0.0 copy-start.1
  304.0 0.0 copy-start.2
  304.1 0.0 copy-done.3
  304.1 0.9 pad_maximum_fusion.1
  305.0 0.5 copy-done.1
  305.5 0.3 copy-done.2
  305.8 2.0 pad_maximum_fusion
  (2 shorter events, 0.0 us)
Async XLA Ops:
  7.2 49.8 %all-gather.11.cloned.1.call-start = ((), (), s32[]{:S(2)}) async-start(), calls=%async_computation.2 | async-start | bytes 2359296 | tf_op jit(solution)/shard_map/all_gather | solution.py:24
  9.2 201.0 %all-reduce.3.cloned.1.call-start = ((), (), s32[]{:S(2)}) async-start(), calls=%async_computation.3 | async-start | bytes 12582912 | tf_op jit(solution)/shard_map/psum | solution.py:23
  29.9 180.3 %copy-start = (bf16[3,2,256,1024]{3,2,1,0:T(8,128)(2,1)S(1)}, bf16[3,2,256,1024]{3,2,1,0:T(8,128)(2,1)}, u32[]{:S(2)}) copy-start(bf16[3,2,256,1024]{3,2,1,0:T(8,128)(2,1)} %param.6) | copy-start | bytes 9437188
  29.9 225.3 %all-gather.9.cloned.1.call-start = ((), (), s32[]{:S(2)}) async-start(), calls=%async_computation.1 | async-start | bytes 2359296 | tf_op jit(solution)/shard_map/all_gather | solution.py:24
  30.7 270.2 %all-gather.7.cloned.1.call-start = ((), (), s32[]{:S(2)}) async-start(), calls=%async_computation | async-start | bytes 2359296 | tf_op jit(solution)/shard_map/all_gather | solution.py:24
  300.9 3.2 %copy-start.3 = (f32[1,2,32,1024]{3,2,1,0:T(8,128)S(1)}, f32[1,2,32,1024]{3,2,1,0:T(8,128)}, u32[]{:S(2)}) copy-start(f32[1,2,32,1024]{3,2,1,0:T(8,128)} %dynamic-slice_bitcast_fusion.1) | copy-start | bytes 786436
  304.0 1.5 copy-start.1
  304.0 1.8 copy-start.2
Sparse Core Ops, SparseCore 0:
  9.8 47.1 all-gather.10
  60.5 149.7 all-reduce.2
  212.0 43.1 all-gather.8
  257.5 43.3 all-gather.6
where the time goes:
time: 315 us; the launch traced here: 314 us
  waiting for transfers between devices  262 us (83%)
  other arithmetic  19.9 us (6%)
  between operations  15.2 us (5%)
  blocking collectives  13.1 us (4%)
  local copies, waits for them, and re-layouts  3.61 us (1%)
    psum x1, waiting for transfers between devices, on_device(): pseudo = lax.psum(term, 'replica')  153 us
    all_gather x3, waiting for transfers between devices, on_device(): moment_full = lax.all_gather(momentum[layer], 'replica', axis=1, tiled=True)  108 us
    psum x1, blocking collectives, on_device(): total = lax.psum(counts[0], 'replica').astype(jnp.float32)  13.1 us
    add x3, other arithmetic, on_device(): moment_next = momentum_rate * moment_full + pseudo  10.8 us
  transfers between devices with their start and end apart: 4, of which 4 were waited for; matrix products, arithmetic and copies ran while one was open for 5% of the time, Pallas kernels for 0%

commit v1 on v0

v1 whole, which is shorter than its diff:
```python
import functools

import jax
import jax.numpy as jnp
from jax import lax
from jax.experimental import pallas as pl
from jax.experimental.pallas import tpu as pltpu
from jax.sharding import PartitionSpec as P

MESH = pl.DeviceIdType.MESH

outer_rate = 0.7
momentum_rate = 0.9

RING = 4
ROWS = 2
ROWS_PER_CHUNK = 16
AHEAD = 2


def tiled(tile, shape):
    wide = jnp.concatenate([tile] * (shape[1] // tile.shape[1]), axis=1)
    return jnp.concatenate([wide] * (shape[0] // tile.shape[0]), axis=0)


def kernel(
    blocks, owned, width,
    counts, inner, anchor, momentum,
    weights_out, momentum_out,
    own, base, moment, got, count, part_sent, part_got, held, gathered, moment_next,
    load_sem, count_send, count_recv, store_sem, weight_sem,
    term_send, term_recv, part_send, part_recv, row_send, row_recv, col_send, col_recv,
):
    me = lax.axis_index("replica")
    row, column = me // RING, me % RING
    other = 1 - row
    across = other * RING + column
    beside = [row * RING + (column + d) % RING for d in range(1, RING)]
    per_block = owned // ROWS_PER_CHUNK
    chunks = blocks * per_block

    def place(c):
        return c // per_block, pl.ds((c % per_block) * ROWS_PER_CHUNK, ROWS_PER_CHUNK)

    def remote(src, dst, send, recv, device):
        return pltpu.make_async_remote_copy(
            src_ref=src,
            dst_ref=dst,
            send_sem=send,
            recv_sem=recv,
            device_id={"replica": device},
            device_id_type=MESH,
        )

    loads = [
        pltpu.make_async_copy(inner.at[:, :, column], own, load_sem.at[0]),
        pltpu.make_async_copy(anchor.at[:, :, column], base, load_sem.at[1]),
        pltpu.make_async_copy(momentum, moment, load_sem.at[2]),
    ]
    for load in loads:
        load.start()
    count[0] = jnp.full(count.shape[1:], counts[0].astype(jnp.float32))

    barrier = pltpu.get_barrier_semaphore()
    for device in [*beside, across]:
        pl.semaphore_signal(
            barrier, inc=1, device_id={"replica": device}, device_id_type=MESH
        )
    pl.semaphore_wait(barrier, RING)

    def count_copy(d):
        return remote(
            count.at[0], count.at[d], count_send.at[d], count_recv.at[d], beside[d - 1]
        )

    def row_count_copy():
        return remote(
            count.at[RING], count.at[RING + 1], count_send.at[0], count_recv.at[0], across
        )

    def term_copy(c, d):
        k, rows = place(c)
        return remote(
            inner.at[k, :, (column + d) % RING, rows],
            got.at[d - 1, k, :, rows],
            term_send.at[c, d - 1],
            term_recv.at[c, d - 1],
            beside[d - 1],
        )

    def part_copy(c):
        k, rows = place(c)
        return remote(
            part_sent.at[k, rows],
            part_got.at[k, rows],
            part_send.at[c],
            part_recv.at[c],
            across,
        )

    def row_copy(c, d):
        k, rows = place(c)
        mine = gathered.at[k, row, column, rows]
        return remote(mine, mine, row_send.at[c, d - 1], row_recv.at[c, d - 1], beside[d - 1])

    def col_copy(c, d):
        k, rows = place(c)
        slab = gathered.at[k, row, (column + RING - d) % RING, rows]
        return remote(slab, slab, col_send.at[c, d], col_recv.at[c, d], across)

    def moment_store(c):
        k, rows = place(c)
        return pltpu.make_async_copy(
            moment_next.at[k, rows], momentum_out.at[k, rows], store_sem.at[c]
        )

    def weight_store(c):
        k, rows = place(c)
        return pltpu.make_async_copy(
            gathered.at[k, :, :, rows], weights_out.at[k, :, :, rows], weight_sem.at[c]
        )

    shape = (ROWS_PER_CHUNK, width)

    def weighted(c, r):
        k, rows = place(c)
        start = base[k, r, rows].astype(jnp.float32)
        total = tiled(count[0], shape) * (start - own[k, r, rows].astype(jnp.float32))
        for d in range(1, RING):
            total = total + tiled(count[d], shape) * (
                start - got[d - 1, k, r, rows].astype(jnp.float32)
            )
        return start, total

    def send_terms(c):
        for d in range(1, RING):
            term_copy(c, d).start()

    def send_part(c):
        for d in range(1, RING):
            term_copy(c, d).wait_recv()
        k, rows = place(c)
        part_sent[k, rows] = weighted(c, other)[1]
        part_copy(c).start()
        held[k, rows] = weighted(c, row)[1]

    def update(c):
        part_copy(c).wait_recv()
        k, rows = place(c)
        start = base[k, row, rows].astype(jnp.float32)
        pseudo = (held[k, rows] + part_got[k, rows]) * tiled(count[RING + 2], shape)
        next_moment = momentum_rate * moment[k, rows] + pseudo
        next_weights = start - outer_rate * (pseudo + momentum_rate * next_moment)
        gathered[k, row, column, rows] = next_weights.astype(gathered.dtype)
        moment_next[k, rows] = next_moment
        for d in range(1, RING):
            row_copy(c, d).start()
        col_copy(c, 0).start()
        moment_store(c).start()

    def forward(c):
        for d in range(1, RING):
            row_copy(c, d).wait_recv()
            col_copy(c, d).start()

    def finish(c):
        for d in range(RING):
            col_copy(c, d).wait_recv()
        weight_store(c).start()

    for d in range(1, RING):
        count_copy(d).start()
    for c in range(min(AHEAD, chunks)):
        send_terms(c)
    for d in range(1, RING):
        count_copy(d).wait_recv()
    count[RING] = count[0] + count[1] + count[2] + count[3]
    row_count_copy().start()
    for load in loads:
        load.wait()

    for t in range(chunks + 4):
        if t < chunks:
            send_part(t)
        if t == 0:
            row_count_copy().wait_recv()
            count[RING + 2] = 1.0 / (count[RING] + count[RING + 1])
        if t + AHEAD < chunks:
            send_terms(t + AHEAD)
        if 0 <= t - 1 < chunks:
            update(t - 1)
        if 0 <= t - 2 < chunks:
            forward(t - 2)
        if 0 <= t - 4 < chunks:
            finish(t - 4)

    for d in range(1, RING):
        count_copy(d).wait_send()
    row_count_copy().wait_send()
    for c in range(chunks):
        for d in range(1, RING):
            term_copy(c, d).wait_send()
            row_copy(c, d).wait_send()
        part_copy(c).wait_send()
        for d in range(RING):
            col_copy(c, d).wait_send()
        moment_store(c).wait()
        weight_store(c).wait()


def on_device(counts, inner, anchor, momentum):
    layers, kinds, owned, width = momentum.shape
    blocks = layers * kinds
    chunks = blocks * (owned // ROWS_PER_CHUNK)
    split = (blocks, ROWS, RING, owned, width)
    dma = pltpu.SemaphoreType.DMA
    anywhere = pl.BlockSpec(memory_space=pl.ANY)
    weights, moments = pl.pallas_call(
        functools.partial(kernel, blocks, owned, width),
        out_shape=(
            jax.ShapeDtypeStruct(split, anchor.dtype),
            jax.ShapeDtypeStruct((blocks, owned, width), momentum.dtype),
        ),
        in_specs=[pl.BlockSpec(memory_space=pltpu.SMEM), anywhere, anywhere, anywhere],
        out_specs=(anywhere, anywhere),
        scratch_shapes=[
            pltpu.VMEM((blocks, ROWS, owned, width), inner.dtype),
            pltpu.VMEM((blocks, ROWS, owned, width), anchor.dtype),
            pltpu.VMEM((blocks, owned, width), jnp.float32),
            pltpu.VMEM((RING - 1, blocks, ROWS, owned, width), inner.dtype),
            pltpu.VMEM((RING + 3, 8, 128), jnp.float32),
            pltpu.VMEM((blocks, owned, width), jnp.float32),
            pltpu.VMEM((blocks, owned, width), jnp.float32),
            pltpu.VMEM((blocks, owned, width), jnp.float32),
            pltpu.VMEM(split, anchor.dtype),
            pltpu.VMEM((blocks, owned, width), jnp.float32),
            dma((3,)),
            dma((RING,)),
            dma((RING,)),
            dma((chunks,)),
            dma((chunks,)),
            dma((chunks, RING - 1)),
            dma((chunks, RING - 1)),
            dma((chunks,)),
            dma((chunks,)),
            dma((chunks, RING - 1)),
            dma((chunks, RING - 1)),
            dma((chunks, RING)),
            dma((chunks, RING)),
        ],
        compiler_params=pltpu.CompilerParams(
            collective_id=0, has_side_effects=True, vmem_limit_bytes=40 << 20
        ),
        name="outer_step",
    )(
        counts,
        inner.reshape(split),
        anchor.reshape(split),
        momentum.reshape(blocks, owned, width),
    )
    return weights.reshape(anchor.shape), moments.reshape(momentum.shape)


def solution(mesh):
    placed = (
        P("replica"),
        P("replica", None, None, "fsdp", None),
        P(None, None, "fsdp", None),
        P(None, None, ("fsdp", "replica"), None),
    )
    return jax.shard_map(
        on_device,
        mesh=mesh,
        in_specs=placed,
        out_specs=(P(None, None, "fsdp", None), P(None, None, ("fsdp", "replica"), None)),
        check_vma=False,
    )
```

time: 315 us -> 78.3 us (0.25)
  waiting for transfers between devices: 262 us -> 0 us
  Pallas kernels: 0 us -> 69.3 us
  other arithmetic: 19.9 us -> 0 us
  between operations: 15.2 us -> 1.29 us
  blocking collectives: 13.1 us -> 0 us
  local copies, waits for them, and re-layouts: 3.61 us -> 7.45 us
    psum x1 -> x0, waiting for transfers between devices: 153 us -> none  [on_device(): pseudo = lax.psum(term, 'replica')]
    all_gather x3 -> x0, waiting for transfers between devices: 108 us -> none  [on_device(): moment_full = lax.all_gather(momentum[layer], 'replica', axis=1, tiled=True)]
    pallas_call x0 -> x1, Pallas kernels: none -> 69.3 us  [on_device(): pl.pallas_call(functools.partial(kernel, blocks, owned, width), out_shape...]
    psum x1 -> x0, blocking collectives: 13.1 us -> none  [on_device(): total = lax.psum(counts[0], 'replica').astype(jnp.float32)]
    add x3 -> x0, other arithmetic: 10.8 us -> none  [on_device(): moment_next = momentum_rate * moment_full + pseudo]
    unnamed x8, local copies, waits for them, and re-layouts: 0.84 us -> 7.45 us
    mul x1 -> x0, other arithmetic: 6.15 us -> none  [on_device(): term = share * (base - inner[0, layer].astype(jnp.float32))]
  transfers between devices with their start and end apart: 4 -> 0, of which waited for: 4 -> 0; matrix products, arithmetic and copies ran while one was open for 5% -> 0% of each run, Pallas kernels for 0% -> 0%
where the time goes in v1:
time: 78.3 us; the launch traced here: 78.1 us
  Pallas kernels  69.3 us (89%)
  local copies, waits for them, and re-layouts  7.45 us (10%)
  between operations  1.29 us (2%)
    pallas_call x1, Pallas kernels, on_device(): pl.pallas_call(functools.partial(kernel, blocks, owned, width), out_shape...  69.3 us
    unnamed x8, local copies, waits for them, and re-layouts  7.45 us

profile of v1, /device:TPU:8, one launch (start us, length us, event | category | flops | bytes accessed | tf_op | source)
XLA Modules:
  0.0 78.1 jit_solution(12459016559068060123)
XLA Ops:
  1.3 0.0 copy-start
  1.3 1.9 %copy-done = bf16[1,3,2,256,1024]{4,3,2,1,0:T(8,128)(2,1)S(1)} copy-done((bf16[1,3,2,256,1024]{4,3,2,1,0:T(8,128)(2,1)S(1)}, bf16[1,3,2,256,1024]{4,3,2,1,0:T(8,128)(2,1)}, u32[]{:S(2)}) %copy-start) | copy-done | bytes 3145752
  3.2 0.0 copy-start.1
  3.2 1.9 %copy-done.1 = bf16[3,2,256,1024]{3,2,1,0:T(8,128)(2,1)S(1)} copy-done((bf16[3,2,256,1024]{3,2,1,0:T(8,128)(2,1)S(1)}, bf16[3,2,256,1024]{3,2,1,0:T(8,128)(2,1)}, u32[]{:S(2)}) %copy-start.1) | copy-done | bytes 3145752
  5.1 0.0 copy-start.2
  5.1 1.1 %copy-done.2 = f32[3,2,32,1024]{3,2,1,0:T(8,128)S(1)} copy-done((f32[3,2,32,1024]{3,2,1,0:T(8,128)S(1)}, f32[3,2,32,1024]{3,2,1,0:T(8,128)}, u32[]{:S(2)}) %copy-start.2) | copy-done | bytes 786456
  6.2 69.3 %outer_step.1 = (bf16[6,2,4,32,1024]{4,3,2,1,0:T(8,128)(2,1)S(1)}, f32[6,32,1024]{2,1,0:T(8,128)S(1)}) custom-call(s32[1]{0:T(128)S(6)} %copy.8.counts, bf16[6,2,4,32,1024]{4,3,2,1,0:T(8,128)(2,1)S(1)} %bitcast.5, bf16[6,2,4,32,1024]{4,3,2,1,0:T(8,128)(2,1)S(1)} %bitcast.6, f32[6,32,1024]{2,1,0:T(8,128)S(1)} %bitcast.8), custom_call_target="tpu_custom_call" | custom-call | tf_op jit(solution)/shard_map/outer_step/pallas_call | solution.py:218
  75.5 1.7 %copy.9 = bf16[3,2,256,1024]{3,2,1,0:T(8,128)(2,1)} copy(bf16[3,2,256,1024]{3,2,1,0:T(8,128)(2,1)S(1)} %bitcast.7) | data formatting | bytes 6291456
  77.2 0.9 %copy.10 = f32[3,2,32,1024]{3,2,1,0:T(8,128)} copy(f32[3,2,32,1024]{3,2,1,0:T(8,128)S(1)} %bitcast.9) | data formatting | bytes 1572864
Async XLA Ops:
  1.3 1.9 %copy-start = (bf16[1,3,2,256,1024]{4,3,2,1,0:T(8,128)(2,1)S(1)}, bf16[1,3,2,256,1024]{4,3,2,1,0:T(8,128)(2,1)}, u32[]{:S(2)}) copy-start(bf16[1,3,2,256,1024]{4,3,2,1,0:T(8,128)(2,1)} %param.5) | copy-start | bytes 9437188
  3.2 1.9 %copy-start.1 = (bf16[3,2,256,1024]{3,2,1,0:T(8,128)(2,1)S(1)}, bf16[3,2,256,1024]{3,2,1,0:T(8,128)(2,1)}, u32[]{:S(2)}) copy-start(bf16[3,2,256,1024]{3,2,1,0:T(8,128)(2,1)} %param.6) | copy-start | bytes 9437188
  5.1 1.1 %copy-start.2 = (f32[3,2,32,1024]{3,2,1,0:T(8,128)S(1)}, f32[3,2,32,1024]{3,2,1,0:T(8,128)}, u32[]{:S(2)}) copy-start(f32[3,2,32,1024]{3,2,1,0:T(8,128)} %param.7) | copy-start | bytes 2359300

commit v2 on v1

v2 whole, which is shorter than its diff:
```python
import functools

import jax
import jax.numpy as jnp
from jax import lax
from jax.experimental import pallas as pl
from jax.experimental.pallas import tpu as pltpu
from jax.sharding import PartitionSpec as P

MESH = pl.DeviceIdType.MESH

outer_rate = 0.7
momentum_rate = 0.9

RING = 4
ROWS = 2
GROUP = 16
PARTS = (1,) * 12
AHEAD = 24.0
UPDATE_LAG = 32.0
RELAY_LAG = 48.0
FORWARD_LAG = 64.0
FINISH_LAG = 96.0
ORDER = "purxfs"
LATE = 96
TURNED = (1, 3)
NEXT = (1, 3)


def chunk_list(blocks, owned, width):
    chunks, done = [], 0.0
    for group in range(blocks * owned // GROUP):
        k, row = divmod(group * GROUP, owned)
        cols = width // PARTS[group]
        for col in range(0, width, cols):
            after = done + GROUP * cols / width
            chunks.append((k, row, GROUP, col, cols, done, after))
            done = after
    return chunks


def schedule(chunks):
    steps = []
    for c, (*_, before, after) in enumerate(chunks):
        steps += [
            (max(before - AHEAD, 0.0), ORDER.index("s"), c, "s"),
            (after, ORDER.index("p"), c, "p"),
            (after + UPDATE_LAG, ORDER.index("u"), c, "u"),
            (after + FORWARD_LAG, ORDER.index("f"), c, "f"),
            (after + RELAY_LAG, ORDER.index("r"), c, "r"),
            (after + RELAY_LAG, ORDER.index("x"), c, "x"),
            (after + FINISH_LAG, len(ORDER), c, "e"),
        ]
    return [(stage, c) for _, _, c, stage in sorted(steps)]


def tiled(tile, shape):
    wide = jnp.concatenate([tile] * (shape[1] // tile.shape[1]), axis=1)
    return jnp.concatenate([wide] * (shape[0] // tile.shape[0]), axis=0)


def kernel(
    blocks, owned, width,
    counts, inner, anchor, momentum,
    gathered, moment_next,
    own, base, moment, got, count, part_sent, part_got, held,
    load_sem, count_send, count_recv,
    term_send, term_recv, part_send, part_recv, row_send, row_recv, col_send, col_recv,
):
    me = lax.axis_index("replica")
    row, column = me // RING, me % RING
    other = 1 - row
    across = other * RING + column
    beside = [row * RING + (column + d) % RING for d in range(1, RING)]
    pieces = chunk_list(blocks, owned, width)
    chunks = len(pieces)

    def place(c):
        k, row, rows, col, cols, _, _ = pieces[c]
        return k, pl.ds(row, rows), pl.ds(col, cols)

    def along_x(c):
        return TURNED if pieces[c][5] >= blocks * owned - LATE else ()

    def remote(src, dst, send, recv, device):
        return pltpu.make_async_remote_copy(
            src_ref=src,
            dst_ref=dst,
            send_sem=send,
            recv_sem=recv,
            device_id={"replica": device},
            device_id_type=MESH,
        )

    loads = [
        pltpu.make_async_copy(inner.at[:, :, column], own, load_sem.at[0]),
        pltpu.make_async_copy(anchor.at[:, :, column], base, load_sem.at[1]),
        pltpu.make_async_copy(momentum, moment, load_sem.at[2]),
    ]
    for load in loads:
        load.start()
    count[0] = jnp.full(count.shape[1:], counts[0].astype(jnp.float32))

    barrier = pltpu.get_barrier_semaphore()
    for device in [*beside, across]:
        pl.semaphore_signal(
            barrier, inc=1, device_id={"replica": device}, device_id_type=MESH
        )
    pl.semaphore_wait(barrier, RING)

    def count_copy(d):
        return remote(
            count.at[0], count.at[d], count_send.at[d], count_recv.at[d], beside[d - 1]
        )

    def row_count_copy():
        return remote(
            count.at[RING], count.at[RING + 1], count_send.at[0], count_recv.at[0], across
        )

    def term_copy(c, d):
        k, rows, cols = place(c)
        return remote(
            inner.at[k, :, (column + d) % RING, rows, cols],
            got.at[d - 1, k, :, rows, cols],
            term_send.at[c, d - 1],
            term_recv.at[c, d - 1],
            beside[d - 1],
        )

    def part_copy(c):
        k, rows, cols = place(c)
        return remote(
            part_sent.at[k, rows, cols],
            part_got.at[k, rows, cols],
            part_send.at[c],
            part_recv.at[c],
            across,
        )

    def row_copy(c, d):
        k, rows, cols = place(c)
        mine = gathered.at[k, row, column, rows, cols]
        return remote(mine, mine, row_send.at[c, d], row_recv.at[c, d], beside[d - 1])

    def relay_copy(c, d):
        k, rows, _ = place(c)
        half = pieces[c][4] // 2
        cols = pl.ds(pieces[c][3] + (0 if d == 1 else half), half)
        slab = gathered.at[k, row, (column + RING - d) % RING, rows, cols]
        return remote(
            slab, slab, row_send.at[c, d - 1], row_recv.at[c, d - 1], beside[d - 1]
        )

    def col_copy(c, d):
        k, rows, cols = place(c)
        slab = gathered.at[k, row, (column + RING - d) % RING, rows, cols]
        return remote(slab, slab, col_send.at[c, d], col_recv.at[c, d], across)

    def turn_copy(c, d):
        k, rows, cols = place(c)
        slab = gathered.at[k, other, column, rows, cols]
        return remote(slab, slab, col_send.at[c, d], col_recv.at[c, d], beside[d - 1])

    def shape(c):
        return pieces[c][2], pieces[c][4]

    def weighted(c, r):
        k, rows, cols = place(c)
        start = base[k, r, rows, cols].astype(jnp.float32)
        total = tiled(count[0], shape(c)) * (start - own[k, r, rows, cols].astype(jnp.float32))
        for d in range(1, RING):
            total = total + tiled(count[d], shape(c)) * (
                start - got[d - 1, k, r, rows, cols].astype(jnp.float32)
            )
        return start, total

    def send_terms(c):
        for d in range(1, RING):
            term_copy(c, d).start()

    def send_part(c):
        for d in range(1, RING):
            term_copy(c, d).wait_recv()
        k, rows, cols = place(c)
        part_sent[k, rows, cols] = weighted(c, other)[1]
        part_copy(c).start()
        held[k, rows, cols] = weighted(c, row)[1]

    def update(c):
        part_copy(c).wait_recv()
        k, rows, cols = place(c)
        start = base[k, row, rows, cols].astype(jnp.float32)
        pseudo = (held[k, rows, cols] + part_got[k, rows, cols]) * tiled(count[RING + 2], shape(c))
        next_moment = momentum_rate * moment[k, rows, cols] + pseudo
        next_weights = start - outer_rate * (pseudo + momentum_rate * next_moment)
        gathered[k, row, column, rows, cols] = next_weights.astype(gathered.dtype)
        moment_next[k, rows, cols] = next_moment
        for d in NEXT:
            row_copy(c, d).start()
        col_copy(c, 0).start()

    def relay(c):
        for d in NEXT:
            row_copy(c, d).wait_recv()
            relay_copy(c, d).start()
            if d not in along_x(c):
                col_copy(c, d).start()

    def forward(c):
        for d in NEXT:
            relay_copy(c, d).wait_recv()
        col_copy(c, 2).start()

    def turn(c):
        col_copy(c, 0).wait_recv()
        for d in along_x(c):
            turn_copy(c, d).start()

    def finish(c):
        for d in range(1, RING):
            col_copy(c, d).wait_recv()

    for d in range(1, RING):
        count_copy(d).start()
    steps = schedule(pieces)
    first = steps.index(("p", 0))
    for stage, c in steps[:first]:
        send_terms(c)
    for d in range(1, RING):
        count_copy(d).wait_recv()
    count[RING] = count[0] + count[1] + count[2] + count[3]
    row_count_copy().start()
    for load in loads:
        load.wait()

    run = {"r": relay, "s": send_terms, "p": send_part, "u": update, "f": forward, "x": turn, "e": finish}
    for stage, c in steps[first:]:
        if stage == "u" and c == 0:
            row_count_copy().wait_recv()
            count[RING + 2] = 1.0 / (count[RING] + count[RING + 1])
        run[stage](c)

    for d in range(1, RING):
        count_copy(d).wait_send()
    row_count_copy().wait_send()
    for c in range(chunks):
        for d in range(1, RING):
            term_copy(c, d).wait_send()
        for d in NEXT:
            row_copy(c, d).wait_send()
            relay_copy(c, d).wait_send()
        part_copy(c).wait_send()
        for d in range(RING):
            col_copy(c, d).wait_send()


def store_kernel(weights, moments, weights_out, moments_out, sem):
    copies = [
        pltpu.make_async_copy(weights, weights_out, sem.at[0]),
        pltpu.make_async_copy(moments, moments_out, sem.at[1]),
    ]
    for copy in copies:
        copy.start()
    for copy in copies:
        copy.wait()


def store(weights, moments):
    anywhere = pl.BlockSpec(memory_space=pl.ANY)
    return pl.pallas_call(
        store_kernel,
        out_shape=(
            jax.ShapeDtypeStruct(weights.shape, weights.dtype),
            jax.ShapeDtypeStruct(moments.shape, moments.dtype),
        ),
        in_specs=[anywhere, anywhere],
        out_specs=(anywhere, anywhere),
        scratch_shapes=[pltpu.SemaphoreType.DMA((2,))],
        compiler_params=pltpu.CompilerParams(vmem_limit_bytes=4 << 20),
        name="store",
    )(weights, moments)


def on_device(counts, inner, anchor, momentum):
    layers, kinds, owned, width = momentum.shape
    blocks = layers * kinds
    chunks = len(chunk_list(blocks, owned, width))
    split = (blocks, ROWS, RING, owned, width)
    dma = pltpu.SemaphoreType.DMA
    anywhere = pl.BlockSpec(memory_space=pltpu.HBM)
    weights, moments = pl.pallas_call(
        functools.partial(kernel, blocks, owned, width),
        out_shape=(
            jax.ShapeDtypeStruct(split, anchor.dtype),
            jax.ShapeDtypeStruct((blocks, owned, width), momentum.dtype),
        ),
        in_specs=[pl.BlockSpec(memory_space=pltpu.SMEM), anywhere, anywhere, anywhere],
        out_specs=(pl.BlockSpec(memory_space=pltpu.VMEM),) * 2,
        scratch_shapes=[
            pltpu.VMEM((blocks, ROWS, owned, width), inner.dtype),
            pltpu.VMEM((blocks, ROWS, owned, width), anchor.dtype),
            pltpu.VMEM((blocks, owned, width), jnp.float32),
            pltpu.VMEM((RING - 1, blocks, ROWS, owned, width), inner.dtype),
            pltpu.VMEM((RING + 3, 8, 128), jnp.float32),
            pltpu.VMEM((blocks, owned, width), jnp.float32),
            pltpu.VMEM((blocks, owned, width), jnp.float32),
            pltpu.VMEM((blocks, owned, width), jnp.float32),
            dma((3,)),
            dma((RING,)),
            dma((RING,)),
            dma((chunks, RING - 1)),
            dma((chunks, RING - 1)),
            dma((chunks,)),
            dma((chunks,)),
            dma((chunks, RING)),
            dma((chunks, RING)),
            dma((chunks, RING)),
            dma((chunks, RING)),
        ],
        compiler_params=pltpu.CompilerParams(
            collective_id=0, has_side_effects=True, vmem_limit_bytes=40 << 20
        ),
        name="outer_step",
    )(
        counts,
        pltpu.with_memory_space_constraint(inner.reshape(split), pltpu.HBM),
        pltpu.with_memory_space_constraint(anchor.reshape(split), pltpu.HBM),
        pltpu.with_memory_space_constraint(momentum.reshape(blocks, owned, width), pltpu.HBM),
    )
    weights, moments = store(weights, moments)
    return weights.reshape(anchor.shape), moments.reshape(momentum.shape)


def solution(mesh):
    placed = (
        P("replica"),
        P("replica", None, None, "fsdp", None),
        P(None, None, "fsdp", None),
        P(None, None, ("fsdp", "replica"), None),
    )
    return jax.shard_map(
        on_device,
        mesh=mesh,
        in_specs=placed,
        out_specs=(P(None, None, "fsdp", None), P(None, None, ("fsdp", "replica"), None)),
        check_vma=False,
    )
```

time: 78.3 us -> 68.5 us (0.87)
  local copies, waits for them, and re-layouts: 7.45 us -> 0 us
  Pallas kernels: 69.3 us -> 67.1 us
    unnamed x8 -> x0, local copies, waits for them, and re-layouts: 7.45 us -> none
    pallas_call x1, Pallas kernels: 69.3 us -> 65.1 us  [on_device(): pl.pallas_call(functools.partial(kernel, blocks, owned, width), out_shape...]
    pallas_call x0 -> x1, Pallas kernels: none -> 1.93 us  [store(): pl.pallas_call(store_kernel, out_shape=(jax.ShapeDtypeStruct(weights.shap...]
where the time goes in v2:
time: 68.5 us; the launch traced here: 68.4 us
  Pallas kernels  67.1 us (98%)
  between operations  1.28 us (2%)
    pallas_call x1, Pallas kernels, on_device(): pl.pallas_call(functools.partial(kernel, blocks, owned, width), out_shape...  65.1 us
    pallas_call x1, Pallas kernels, store(): pl.pallas_call(store_kernel, out_shape=(jax.ShapeDtypeStruct(weights.shap...  1.93 us

profile of v2, /device:TPU:8, one launch (start us, length us, event | category | flops | bytes accessed | tf_op | source)
XLA Modules:
  0.0 68.4 jit_solution(2695873331060792560)
XLA Ops:
  1.3 65.1 %outer_step.1 = (bf16[6,2,4,32,1024]{4,3,2,1,0:T(8,128)(2,1)S(1)}, f32[6,32,1024]{2,1,0:T(8,128)S(1)}) custom-call(s32[1]{0:T(128)S(6)} %copy.6.counts, bf16[6,2,4,32,1024]{4,3,2,1,0:T(8,128)(2,1)} %bitcast.5, bf16[6,2,4,32,1024]{4,3,2,1,0:T(8,128)(2,1)} %bitcast.6, f32[6,32,1024]{2,1,0:T(8,128)} %bitcast.7), custom_call_target="tpu_custom_call" | custom-call | tf_op jit(solution)/shard_map/outer_step/pallas_call | solution.py:292
  66.4 1.9 %store.1 = (bf16[6,2,4,32,1024]{4,3,2,1,0:T(8,128)(2,1)}, f32[6,32,1024]{2,1,0:T(8,128)}) custom-call(bf16[6,2,4,32,1024]{4,3,2,1,0:T(8,128)(2,1)S(1)} %get-tuple-element.6.weights, f32[6,32,1024]{2,1,0:T(8,128)S(1)} %get-tuple-element.7.moments), custom_call_target="tpu_custom_call" | custom-call | tf_op jit(solution)/shard_map/store/pallas_call | solution.py:271

commit v3 on v2

--- a/solution.py
+++ b/solution.py
@@ -14,28 +14,24 @@
 
 RING = 4
 ROWS = 2
-GROUP = 16
-PARTS = (1,) * 12
-AHEAD = 24.0
-UPDATE_LAG = 32.0
-RELAY_LAG = 48.0
-FORWARD_LAG = 64.0
-FINISH_LAG = 96.0
+SIZES = (16,) * 12
+AHEAD = 32.0
+UPDATE_LAG = 24.0
+RELAY_LAG = 56.0
+FORWARD_LAG = 88.0
+FINISH_LAG = 120.0
 ORDER = "purxfs"
 LATE = 96
 TURNED = (1, 3)
 NEXT = (1, 3)
 
 
-def chunk_list(blocks, owned, width):
-    chunks, done = [], 0.0
-    for group in range(blocks * owned // GROUP):
-        k, row = divmod(group * GROUP, owned)
-        cols = width // PARTS[group]
-        for col in range(0, width, cols):
-            after = done + GROUP * cols / width
-            chunks.append((k, row, GROUP, col, cols, done, after))
-            done = after
+def chunk_list(owned, width):
+    chunks, done = [], 0
+    for rows in SIZES:
+        k, row = divmod(done, owned)
+        chunks.append((k, row, rows, 0, width, done, done + rows))
+        done += rows
     return chunks
 
 
@@ -72,7 +68,7 @@
     other = 1 - row
     across = other * RING + column
     beside = [row * RING + (column + d) % RING for d in range(1, RING)]
-    pieces = chunk_list(blocks, owned, width)
+    pieces = chunk_list(owned, width)
     chunks = len(pieces)
 
     def place(c):
@@ -285,7 +281,7 @@
 def on_device(counts, inner, anchor, momentum):
     layers, kinds, owned, width = momentum.shape
     blocks = layers * kinds
-    chunks = len(chunk_list(blocks, owned, width))
+    chunks = len(chunk_list(owned, width))
     split = (blocks, ROWS, RING, owned, width)
     dma = pltpu.SemaphoreType.DMA
     anywhere = pl.BlockSpec(memory_space=pltpu.HBM)

time: 68.5 us -> 67 us (0.978)
  Pallas kernels: 67.1 us -> 65.1 us
    pallas_call x1, Pallas kernels: 65.1 us -> 63.1 us  [on_device(): pl.pallas_call(functools.partial(kernel, blocks, owned, width), out_shape...]
where the time goes in v3:
time: 67 us; the launch traced here: 66.3 us
  Pallas kernels  65.1 us (97%)
  between operations  1.28 us (2%)
    pallas_call x1, Pallas kernels, on_device(): pl.pallas_call(functools.partial(kernel, blocks, owned, width), out_shape...  63.1 us
    pallas_call x1, Pallas kernels, store(): pl.pallas_call(store_kernel, out_shape=(jax.ShapeDtypeStruct(weights.shap...  1.93 us

profile of v3, /device:TPU:8, one launch (start us, length us, event | category | flops | bytes accessed | tf_op | source)
XLA Modules:
  0.0 66.3 jit_solution(10593173409042052030)
XLA Ops:
  1.3 63.1 %outer_step.1 = (bf16[6,2,4,32,1024]{4,3,2,1,0:T(8,128)(2,1)S(1)}, f32[6,32,1024]{2,1,0:T(8,128)S(1)}) custom-call(s32[1]{0:T(128)S(6)} %copy.6.counts, bf16[6,2,4,32,1024]{4,3,2,1,0:T(8,128)(2,1)} %bitcast.5, bf16[6,2,4,32,1024]{4,3,2,1,0:T(8,128)(2,1)} %bitcast.6, f32[6,32,1024]{2,1,0:T(8,128)} %bitcast.7), custom_call_target="tpu_custom_call" | custom-call | tf_op jit(solution)/shard_map/outer_step/pallas_call | solution.py:288
  64.4 1.9 %store.1 = (bf16[6,2,4,32,1024]{4,3,2,1,0:T(8,128)(2,1)}, f32[6,32,1024]{2,1,0:T(8,128)}) custom-call(bf16[6,2,4,32,1024]{4,3,2,1,0:T(8,128)(2,1)S(1)} %get-tuple-element.6.weights, f32[6,32,1024]{2,1,0:T(8,128)S(1)} %get-tuple-element.7.moments), custom_call_target="tpu_custom_call" | custom-call | tf_op jit(solution)/shard_map/store/pallas_call | solution.py:267

commit v4 on v3

--- a/solution.py
+++ b/solution.py
@@ -18,8 +18,9 @@
 AHEAD = 32.0
 UPDATE_LAG = 24.0
 RELAY_LAG = 56.0
+TURN_LAG = 72.0
 FORWARD_LAG = 88.0
-FINISH_LAG = 120.0
+FINISH_LAG = 1000.0
 ORDER = "purxfs"
 LATE = 96
 TURNED = (1, 3)
@@ -44,7 +45,7 @@
             (after + UPDATE_LAG, ORDER.index("u"), c, "u"),
             (after + FORWARD_LAG, ORDER.index("f"), c, "f"),
             (after + RELAY_LAG, ORDER.index("r"), c, "r"),
-            (after + RELAY_LAG, ORDER.index("x"), c, "x"),
+            (after + TURN_LAG, ORDER.index("x"), c, "x"),
             (after + FINISH_LAG, len(ORDER), c, "e"),
         ]
     return [(stage, c) for _, _, c, stage in sorted(steps)]
@@ -88,6 +89,11 @@
             device_id_type=MESH,
         )
 
+    barrier = pltpu.get_barrier_semaphore()
+    for device in [*beside, across]:
+        pl.semaphore_signal(
+            barrier, inc=1, device_id={"replica": device}, device_id_type=MESH
+        )
     loads = [
         pltpu.make_async_copy(inner.at[:, :, column], own, load_sem.at[0]),
         pltpu.make_async_copy(anchor.at[:, :, column], base, load_sem.at[1]),
@@ -97,11 +103,6 @@
         load.start()
     count[0] = jnp.full(count.shape[1:], counts[0].astype(jnp.float32))
 
-    barrier = pltpu.get_barrier_semaphore()
-    for device in [*beside, across]:
-        pl.semaphore_signal(
-            barrier, inc=1, device_id={"replica": device}, device_id_type=MESH
-        )
     pl.semaphore_wait(barrier, RING)
 
     def count_copy(d):
@@ -192,9 +193,9 @@
         next_weights = start - outer_rate * (pseudo + momentum_rate * next_moment)
         gathered[k, row, column, rows, cols] = next_weights.astype(gathered.dtype)
         moment_next[k, rows, cols] = next_moment
+        col_copy(c, 0).start()
         for d in NEXT:
             row_copy(c, d).start()
-        col_copy(c, 0).start()
 
     def relay(c):
         for d in NEXT:

time: 67 us -> 67.1 us (level)
  no operation moved by 1% of the time
where the time goes in v4:
time: 67.1 us; the launch traced here: 66.2 us
  Pallas kernels  64.9 us (97%)
  between operations  1.28 us (2%)
    pallas_call x1, Pallas kernels, on_device(): pl.pallas_call(functools.partial(kernel, blocks, owned, width), out_shape...  63 us
    pallas_call x1, Pallas kernels, store(): pl.pallas_call(store_kernel, out_shape=(jax.ShapeDtypeStruct(weights.shap...  1.93 us

profile of v4, /device:TPU:8, one launch (start us, length us, event | category | flops | bytes accessed | tf_op | source)
XLA Modules:
  0.0 66.2 jit_solution(7940308087744678339)
XLA Ops:
  1.3 63.0 %outer_step.1 = (bf16[6,2,4,32,1024]{4,3,2,1,0:T(8,128)(2,1)S(1)}, f32[6,32,1024]{2,1,0:T(8,128)S(1)}) custom-call(s32[1]{0:T(128)S(6)} %copy.6.counts, bf16[6,2,4,32,1024]{4,3,2,1,0:T(8,128)(2,1)} %bitcast.5, bf16[6,2,4,32,1024]{4,3,2,1,0:T(8,128)(2,1)} %bitcast.6, f32[6,32,1024]{2,1,0:T(8,128)} %bitcast.7), custom_call_target="tpu_custom_call" | custom-call | tf_op jit(solution)/shard_map/outer_step/pallas_call | solution.py:289
  64.3 1.9 %store.1 = (bf16[6,2,4,32,1024]{4,3,2,1,0:T(8,128)(2,1)}, f32[6,32,1024]{2,1,0:T(8,128)}) custom-call(bf16[6,2,4,32,1024]{4,3,2,1,0:T(8,128)(2,1)S(1)} %get-tuple-element.6.weights, f32[6,32,1024]{2,1,0:T(8,128)S(1)} %get-tuple-element.7.moments), custom_call_target="tpu_custom_call" | custom-call | tf_op jit(solution)/shard_map/store/pallas_call | solution.py:268

commit v5 on v4

--- a/solution.py
+++ b/solution.py
@@ -253,10 +253,11 @@
 
 
 def store_kernel(weights, moments, weights_out, moments_out, sem):
-    copies = [
-        pltpu.make_async_copy(weights, weights_out, sem.at[0]),
-        pltpu.make_async_copy(moments, moments_out, sem.at[1]),
-    ]
+    copies = [pltpu.make_async_copy(moments, moments_out, sem.at[0])]
+    for k in range(weights.shape[0]):
+        copies.append(
+            pltpu.make_async_copy(weights.at[k], weights_out.at[k], sem.at[k + 1])
+        )
     for copy in copies:
         copy.start()
     for copy in copies:
@@ -273,7 +274,7 @@
         ),
         in_specs=[anywhere, anywhere],
         out_specs=(anywhere, anywhere),
-        scratch_shapes=[pltpu.SemaphoreType.DMA((2,))],
+        scratch_shapes=[pltpu.SemaphoreType.DMA((weights.shape[0] + 1,))],
         compiler_params=pltpu.CompilerParams(vmem_limit_bytes=4 << 20),
         name="store",
     )(weights, moments)

time: 67.1 us -> 67.1 us (level)
  no operation moved by 1% of the time
where the time goes in v5:
time: 67.1 us; the launch traced here: 66.3 us
  Pallas kernels  65 us (97%)
  between operations  1.28 us (2%)
    pallas_call x1, Pallas kernels, on_device(): pl.pallas_call(functools.partial(kernel, blocks, owned, width), out_shape...  63 us
    pallas_call x1, Pallas kernels, store(): pl.pallas_call(store_kernel, out_shape=(jax.ShapeDtypeStruct(weights.shap...  1.98 us

profile of v5, /device:TPU:8, one launch (start us, length us, event | category | flops | bytes accessed | tf_op | source)
XLA Modules:
  0.0 66.3 jit_solution(16819781574071559759)
XLA Ops:
  1.3 63.0 %outer_step.1 = (bf16[6,2,4,32,1024]{4,3,2,1,0:T(8,128)(2,1)S(1)}, f32[6,32,1024]{2,1,0:T(8,128)S(1)}) custom-call(s32[1]{0:T(128)S(6)} %copy.6.counts, bf16[6,2,4,32,1024]{4,3,2,1,0:T(8,128)(2,1)} %bitcast.5, bf16[6,2,4,32,1024]{4,3,2,1,0:T(8,128)(2,1)} %bitcast.6, f32[6,32,1024]{2,1,0:T(8,128)} %bitcast.7), custom_call_target="tpu_custom_call" | custom-call | tf_op jit(solution)/shard_map/outer_step/pallas_call | solution.py:290
  64.3 2.0 %store.1 = (bf16[6,2,4,32,1024]{4,3,2,1,0:T(8,128)(2,1)}, f32[6,32,1024]{2,1,0:T(8,128)}) custom-call(bf16[6,2,4,32,1024]{4,3,2,1,0:T(8,128)(2,1)S(1)} %get-tuple-element.6.weights, f32[6,32,1024]{2,1,0:T(8,128)S(1)} %get-tuple-element.7.moments), custom_call_target="tpu_custom_call" | custom-call | tf_op jit(solution)/shard_map/store/pallas_call | solution.py:269
